TPU v7x, 256 devices: a whole 4x4x8 slice. The times are simulated.
256 devices in a mesh: rows: 64 (over y, z, core), feat: 4 (over x).
Axes of the slice: x: 4, y: 4, z: 8, core: 2. Of those that a mesh axis runs over, the one named last changes fastest.
Arguments:
- cells: bfloat16 [8192, 80, 128], P('rows', 'feat'), may hold values from -19 to 19
- block_table: int32 [64], replicated, may hold values from 0 to 7, as said below
- row_live: int32 [8192], replicated, may hold values from 0 to 1, as said below
- row_train: int32 [8192], replicated, may hold values from 0 to 1, as said below
- feat_qkv: bfloat16 [128, 384], replicated, may hold values from -0.5 to 0.5
- feat_out: bfloat16 [128, 128], replicated, may hold values from -0.5 to 0.5
- item_qkv: bfloat16 [128, 384], replicated, may hold values from -0.5 to 0.5
- item_out: bfloat16 [128, 128], replicated, may hold values from -0.5 to 0.5
Outputs:
- layer_output: bfloat16 [8192, 80, 128], P(('rows', 'feat'))
Inputs may be any that keep to these rules, and one draw needn't show every extreme that they name: `block_table`: every table number appears in some block. `row_live`: every training row is live. `row_train`: each aligned group of 32 rows holds 1 to 4 training rows; some group holds exactly 4.
All inputs are finite; a program needn't handle non-finite values.
Results may differ from a plain program's by a relative error of at most 0.014.
Values may be sent and summed in bfloat16 or wider, within the bound.
A program may use at most 64 MiB of HBM per device.

v0:
```python
import jax
import jax.numpy as jnp
from jax import lax
from jax.sharding import PartitionSpec as P

HEADS = 4
HEAD_DIM = 32
KEEP = 4
TABLES = 8
EPSILON = 1e-05
MASKED = -1e30


def from_everyone(shard, axis):
    peers = lax.axis_size(axis)
    return lax.all_to_all(
        jnp.broadcast_to(shard[None], (peers, *shard.shape)), axis, 0, 0, tiled=True
    )


def of_everyone(shard, axis):
    everything = from_everyone(shard, axis)
    return jnp.sum(everything, axis=0)


def in_one(arrays, axis):
    vector, at, done = (jnp.concatenate([a.reshape(-1) for a in arrays]), 0, [])
    so_far = of_everyone(vector, axis)
    for a in arrays:
        done.append(so_far[at : at + a.size].reshape(a.shape))
        at += a.size
    return tuple(done)


def laid_out(parts, dim):
    lengths = list(parts.shape[1:])
    lengths[dim] *= parts.shape[0]
    return jnp.moveaxis(parts, 0, dim).reshape(lengths)


def gather_together(arrays, axis, dims):
    vector = jnp.concatenate([a.reshape(-1) for a in arrays])
    lines, at, done = (lax.all_gather(vector, axis), 0, [])
    for a, dim in zip(arrays, dims):
        parts = lines[:, at : at + a.size].reshape(-1, *a.shape)
        done.append(laid_out(parts, dim))
        at += a.size
    return tuple(done)


def compact_train(train_rows):
    positions = jnp.arange(train_rows.shape[-1], dtype=jnp.int32)
    ordinal = jnp.cumsum(train_rows, axis=-1) - 1
    slot_ids = jnp.arange(KEEP, dtype=jnp.int32)
    matched = (train_rows[..., None, :] == 1) & (ordinal[..., None, :] == slot_ids[:, None])
    return jnp.sum(jnp.where(matched, positions, 0), axis=-1)


def into_heads(tensor):
    return tensor.reshape(tensor.shape[:-1] + (HEADS, HEAD_DIM))


def attend_features(queries, key_part, value_part):
    row_count, query_feats = (queries.shape[0], queries.shape[1])
    blocks = max(1, row_count * query_feats // 1280)
    while row_count % blocks:
        blocks -= 1
    scaling = HEAD_DIM ** (-0.5)

    def attend_one_block(block_parts):
        block_query, block_key, block_value = block_parts
        scores = (
            jnp.einsum(
                "rqhd,rkhd->rhqk", block_query, block_key, preferred_element_type=jnp.float32
            )
            * scaling
        )
        shares = jax.nn.softmax(scores, axis=-1).astype(jnp.bfloat16)
        return jnp.einsum(
            "rhqk,rkhd->rqhd", shares, block_value, preferred_element_type=jnp.float32
        ).astype(jnp.bfloat16)

    def by_block(tensor):
        return tensor.reshape((blocks, row_count // blocks) + tensor.shape[1:])

    result = lax.map(
        attend_one_block, (by_block(queries), by_block(key_part), by_block(value_part))
    )
    return result.reshape(row_count, query_feats, HEADS * HEAD_DIM)


def feature_layer(normed_cells, feat_out, key_part, value_part, queries):
    attended = attend_features(queries, key_part, value_part)
    update = jnp.dot(attended, feat_out, preferred_element_type=jnp.float32)
    return (normed_cells.astype(jnp.float32) + update).astype(jnp.bfloat16)


def on_device(cells, block_table, row_live, row_train, feat_qkv, feat_out, item_qkv, item_out):
    rows_here, feats_here, width_all = cells.shape
    row_index = lax.axis_index("rows")
    feat_index = lax.axis_index("feat")
    row_devices = lax.axis_size("rows")
    feat_devices = lax.axis_size("feat")
    my_table = lax.dynamic_index_in_dim(block_table, row_index, keepdims=False)
    live_rows = lax.dynamic_slice_in_dim(row_live, row_index * rows_here, rows_here).astype(
        jnp.float32
    )
    values = cells.astype(jnp.float32)
    table_hot = (jnp.arange(TABLES, dtype=jnp.int32) == my_table).astype(jnp.float32)
    first_local = jnp.sum(values * live_rows[:, None, None], axis=(0, 2))
    count_local = jnp.sum(live_rows) * width_all
    second_local = jnp.sum(values * values * live_rows[:, None, None], axis=(0, 2))
    first_sum, second_sum, count_sum = in_one(
        (
            table_hot[:, None] * first_local[None, :],
            table_hot[:, None] * second_local[None, :],
            table_hot * count_local,
        ),
        "rows",
    )
    table_mean = first_sum / count_sum[:, None]
    table_spread = second_sum / count_sum[:, None] - table_mean * table_mean
    mine_mean = lax.dynamic_index_in_dim(table_mean, my_table, keepdims=False)
    centred = values - mine_mean[None, :, None]
    mine_spread = lax.dynamic_index_in_dim(table_spread, my_table, keepdims=False)
    normed = (centred * lax.rsqrt(mine_spread + EPSILON)[None, :, None]).astype(jnp.bfloat16)
    normed_rows = lax.all_to_all(normed, "feat", split_axis=0, concat_axis=1, tiled=True)
    projected = jnp.dot(normed_rows, feat_qkv, preferred_element_type=jnp.float32).astype(
        jnp.bfloat16
    )
    queries = into_heads(projected[..., :width_all])
    key_part = into_heads(projected[..., width_all : 2 * width_all])
    value_part = into_heads(projected[..., 2 * width_all :])
    mixed_rows = feature_layer(normed_rows, feat_out, key_part, value_part, queries)
    group_rows, total_feats = (mixed_rows.shape[0], mixed_rows.shape[1])
    per_device = total_feats * HEADS // row_devices
    first_row = row_index * rows_here + feat_index * group_rows
    train_here = lax.dynamic_slice_in_dim(row_train, first_row, group_rows)
    places = compact_train(train_here)
    chosen = jnp.take(mixed_rows, places, axis=0)
    item_query = jnp.dot(
        mixed_rows, item_qkv[:, :width_all], preferred_element_type=jnp.float32
    ).astype(jnp.bfloat16)
    item_query = item_query.reshape(group_rows, row_devices, per_device, HEAD_DIM)
    key_value = jnp.dot(chosen, item_qkv[:, width_all:], preferred_element_type=jnp.float32).astype(
        jnp.bfloat16
    )
    item_key = key_value[..., :width_all].reshape(KEEP, row_devices, per_device, HEAD_DIM)
    item_value = key_value[..., width_all:].reshape(KEEP, row_devices, per_device, HEAD_DIM)
    query_table = jnp.repeat(block_table, group_rows)
    groups_all = row_train.reshape(row_devices, feat_devices, group_rows)
    group_counts = jnp.sum(groups_all, axis=2)
    slot_ids = jnp.arange(KEEP, dtype=jnp.int32)
    key_valid = slot_ids[None, None, :] < jnp.transpose(group_counts)[:, :, None]
    key_table = jnp.broadcast_to(block_table[None, :, None], key_valid.shape)
    allowed = (query_table[:, None] == key_table.reshape(-1)[None, :]) & key_valid.reshape(-1)[
        None, :
    ]
    query_count = query_table.shape[0]
    key_count = allowed.shape[1]
    query_blocks = max(1, query_count // 512)
    while query_count % query_blocks:
        query_blocks -= 1
    scaling = HEAD_DIM ** (-0.5)
    blocked_allowed = allowed.reshape(query_blocks, query_count // query_blocks, key_count)
    local_query = lax.all_to_all(item_query, "rows", split_axis=1, concat_axis=0, tiled=True)
    local_key = lax.all_to_all(item_key, "rows", split_axis=1, concat_axis=0, tiled=True)
    local_value = lax.all_to_all(item_value, "rows", split_axis=1, concat_axis=0, tiled=True)
    every_key, every_value = gather_together((local_key, local_value), "feat", (0, 0))

    def one_item(item_parts):
        single_query, single_key, single_value = item_parts

        def one_one_block(block_parts):
            block_query, block_allowed = block_parts
            scores = (
                jnp.dot(block_query, single_key.T, preferred_element_type=jnp.float32) * scaling
            )
            scores = jnp.where(block_allowed, scores, MASKED)
            shares = jax.nn.softmax(scores, axis=-1).astype(jnp.bfloat16)
            return jnp.dot(shares, single_value, preferred_element_type=jnp.float32).astype(
                jnp.bfloat16
            )

        blocked_query = single_query.reshape(query_blocks, query_count // query_blocks, HEAD_DIM)
        return lax.map(one_one_block, (blocked_query, blocked_allowed)).reshape(
            query_count, HEAD_DIM
        )

    by_item = (
        jnp.moveaxis(local_query[:, 0], 1, 0),
        jnp.moveaxis(every_key[:, 0], 1, 0),
        jnp.moveaxis(every_value[:, 0], 1, 0),
    )
    result = jnp.moveaxis(lax.map(one_item, by_item), 0, 1)[:, None]
    attended = lax.all_to_all(result, "rows", split_axis=0, concat_axis=1, tiled=True)
    attended = attended.reshape(group_rows, total_feats, width_all)
    update = jnp.dot(attended, item_out, preferred_element_type=jnp.float32)
    return (mixed_rows.astype(jnp.float32) + update).astype(jnp.bfloat16)


def solution(mesh):
    return jax.shard_map(
        on_device,
        mesh=mesh,
        in_specs=(P("rows", "feat", None), P(), P(), P(), P(), P(), P(), P()),
        out_specs=P(("rows", "feat"), None, None),
        check_vma=False,
    )
```

profile of v0, /device:TPU:1, one launch (start us, length us, event | category | flops | bytes accessed | tf_op | source)
XLA Modules:
  0.0 263.0 jit_solution(8148468147780909118)
XLA Ops:
  0.0 1.4 dynamic_slice.46
  2.1 1.4 fusion.48
  3.5 1.7 fusion.27
  7.5 13.1 %all-to-all-start = ((f32[64,1,328]{2,1,0:T(1,128)}), f32[64,1,328]{2,1,0:T(1,128)S(1)}, u32[]{:S(2)}, u32[]{:S(2)}) async-start(f32[64,1,328]{2,1,0:T(1,128)} %broadcast_in_dim.81), calls=%async_computation | async-start | bytes 196608 | tf_op jit(solution)/shard_map/all_to_all | solution.py:16
  20.7 0.9 reshape.170
  22.6 1.2 reduce_sum.80
  28.9 2.0 all-to-all-done
  31.4 1.3 fusion.31
  32.7 4.0 %all-to-all-start.1 = ((bf16[128,20,128]{2,1,0:T(8,128)(2,1)}), bf16[128,20,128]{2,1,0:T(8,128)(2,1)S(1)}, u32[]{:S(2)}, u32[]{:S(2)}) async-start(bf16[128,20,128]{2,1,0:T(8,128)(2,1)} %fusion.31), calls=%async_computation.1 | async-start | bytes 1572864 | tf_op jit(solution)/shard_map/all_to_all | solution.py:127
  36.8 11.7 %all-to-all-done.1 = bf16[128,20,128]{2,1,0:T(8,128)(2,1)S(1)} async-done(((bf16[128,20,128]{2,1,0:T(8,128)(2,1)}), bf16[128,20,128]{2,1,0:T(8,128)(2,1)S(1)}, u32[]{:S(2)}, u32[]{:S(2)}) %all-to-all-start.1) | async-done | bytes 655392 | tf_op jit(solution)/shard_map/all_to_all | solution.py:127
  49.6 1.3 copy.106
  52.2 10.6 %while.32 = (s32[]{:T(128)}, bf16[2,16,80,4,32]{2,4,3,1,0:T(8,128)(2,1)}, bf16[2,16,80,4,32]{2,4,3,1,0:T(8,128)(2,1)}, bf16[2,16,80,4,32]{2,4,3,1,0:T(8,128)(2,1...) while((s32[]{:T(128)}, bf16[2,16,80,4,32]{2,4,3,1,0:T(8,128)(2,1)}, ...), condition=%wide.region_7.8_spmd, body=%wide.region_4.7_spmd.sunk | while | flops 55050320 | bytes 12310625 | solution.py:86
  52.8 3.4 %fusion.75 = (f32[16,4,80]{2,1,0:T(4,128)S(1)}, f32[16,4,80,80]{2,3,1,0:T(8,128)S(1)}) fusion(f32[16,4,80,80]{2,3,1,0:T(8,128)S(1)} %fusion.74), kind=kOutput, calls=%fused_computation.90.clone.1 | output fusion | flops 1638479 | bytes 3297280 | tf_op jit(solution)/shard_map/while/body/eval_jaxpr/sub | solution.py:78
  56.2 1.3 fusion.76
  58.1 3.4 %fusion.75 = (f32[16,4,80]{2,1,0:T(4,128)S(1)}, f32[16,4,80,80]{2,3,1,0:T(8,128)S(1)}) fusion(f32[16,4,80,80]{2,3,1,0:T(8,128)S(1)} %fusion.74), kind=kOutput, calls=%fused_computation.90.clone.1 | output fusion | flops 1638479 | bytes 3297280 | tf_op jit(solution)/shard_map/while/body/eval_jaxpr/sub | solution.py:78
  61.5 1.3 fusion.76
  62.8 1.7 fusion.32
  66.2 0.9 reshape.192
  67.1 9.5 %all-to-all-start.3 = ((bf16[64,2,320]{2,1,0:T(2,128)(2,1)}), bf16[64,2,320]{2,1,0:T(2,128)(2,1)S(1)}, u32[]{:S(2)}, u32[]{:S(2)}) async-start(bf16[64,2,320]{2,1,0:T(2,128)(2,1)} %reshape.192), calls=%async_computation.3 | async-start | bytes 196608 | tf_op jit(solution)/shard_map/all_to_all | solution.py:167
  77.3 0.9 reshape.190
  78.5 3.8 %reshape.164 = bf16[32,64,5,32]{3,2,1,0:T(8,128)(2,1)} reshape(bf16[32,80,128]{2,1,0:T(8,128)(2,1)S(1)} %convolution_convert_fusion.2) | data formatting | bytes 1310720 | tf_op jit(solution)/shard_map/reshape | solution.py:144
  82.4 5.2 %copy.144 = bf16[32,64,5,32]{3,0,2,1:T(8,128)(2,1)S(1)} copy(bf16[32,64,5,32]{3,2,1,0:T(8,128)(2,1)} %reshape.164) | data formatting | bytes 1310720 | tf_op jit(solution)/shard_map/reshape | solution.py:144
  87.6 2.6 reshape.188
  90.2 10.3 %all-to-all-start.4 = ((bf16[64,2,320]{2,1,0:T(2,128)(2,1)}), bf16[64,2,320]{2,1,0:T(2,128)(2,1)S(1)}, u32[]{:S(2)}, u32[]{:S(2)}) async-start(bf16[64,2,320]{2,1,0:T(2,128)(2,1)} %reshape.190), calls=%async_computation.4 | async-start | bytes 196608 | tf_op jit(solution)/shard_map/all_to_all | solution.py:168
  101.3 9.4 %all-to-all-done.4 = bf16[64,2,320]{2,1,0:T(2,128)(2,1)S(1)} async-done(((bf16[64,2,320]{2,1,0:T(2,128)(2,1)}), bf16[64,2,320]{2,1,0:T(2,128)(2,1)S(1)}, u32[]{:S(2)}, u32[]{:S(2)}) %all-to-all-start.4) | async-done | bytes 81952 | tf_op jit(solution)/shard_map/all_to_all | solution.py:168
  110.7 4.5 %all-to-all-start.2 = ((bf16[64,2,2560]{2,1,0:T(2,128)(2,1)}), bf16[64,2,2560]{2,1,0:T(2,128)(2,1)S(1)}, u32[]{:S(2)}, u32[]{:S(2)}) async-start(bf16[64,2,2560]{2,1,0:T(2,128)(2,1)} %reshape.188), calls=%async_computation.2 | async-start | bytes 1310720 | tf_op jit(solution)/shard_map/all_to_all | solution.py:166
  116.0 11.3 %all-gather = bf16[327680]{0:T(1024)(128)(2,1)S(1)} all-gather(bf16[81920]{0:T(1024)(128)(2,1)S(1)} %pad_maximum_fusion), channel_id=2, replica_groups=mesh['rows'=64,'feat'=4] {'feat'}, dimensions={0}, use_global_device_ids=true | all-gather | bytes 819200 | tf_op jit(solution)/shard_map/all_gather | solution.py:43
  127.5 1.0 fusion.52
  128.4 2.3 squeeze_reshape_reshape.6
  130.8 1.3 copy.119
  132.1 1.4 squeeze_reshape_reshape.7
  133.5 1.2 copy.120
  135.3 1.4 reshape.189
  136.7 2.0 bitcast_bitcast_fusion
  138.7 3.9 %copy.111 = bf16[64,32,1,5,32]{1,0,4,3,2:T(8,128)(2,1)S(1)} copy(bf16[64,32,1,5,32]{4,1,3,0,2:T(8,128)(2,1)} %bitcast_bitcast_fusion) | data formatting | bytes 1310720 | tf_op jit(solution)/shard_map/all_to_all | solution.py:166
  142.6 3.5 %squeeze.38 = bf16[2048,5,32]{0,2,1:T(8,128)(2,1)} reshape(bf16[64,32,1,5,32]{1,0,4,3,2:T(8,128)(2,1)S(1)} %copy.111) | data formatting | bytes 1310720 | tf_op jit(solution)/shard_map/squeeze | solution.py:191
  146.1 59.1 %while.34 = (s32[]{:T(128)}, bf16[5,2048,32]{2,1,0:T(8,128)(2,1)}, bf16[5,2048,32]{1,2,0:T(8,128)(2,1)}, bf16[5,1024,32]{2,1,0:T(8,128)(2,1)}, bf16[5,1024,32]{2...) while((s32[]{:T(128)}, bf16[5,2048,32]{2,1,0:T(8,128)(2,1)}, ...), condition=%wide.region_16.17_spmd.clone, body=%wide.region_11.16_spmd.clone.sunk | while | flops 75512832 | bytes 11330310 | solution.py:195
  146.1 1.1 dynamic-slice_bitcast_fusion.5
  147.1 0.9 constant_dynamic-slice_fusion.2
  148.3 1.5 compare_and_fusion.3
  149.9 6.9 %while.35 = (s32[]{:T(128)}, bf16[4,512,32]{1,2,0:T(8,128)(2,1)S(1)}, pred[4,512,1024]{2,1,0:T(32,128)(4,1)S(1)}, bf16[4,512,32]{2,1,0:T(8,128)(2,1)S(1)}, bf16[...) while((s32[]{:T(128)}, bf16[4,512,32]{1,2,0:T(8,128)(2,1)S(1)}, ...), condition=%wide.region_15.15_spmd, body=%wide.region_12.14_spmd.sunk | while | flops 71318528 | bytes 7515217 | solution.py:186
  157.9 1.1 dynamic-slice_bitcast_fusion.5
  158.9 0.9 constant_dynamic-slice_fusion.2
  160.1 1.5 compare_and_fusion.3
  161.7 6.9 %while.35 = (s32[]{:T(128)}, bf16[4,512,32]{1,2,0:T(8,128)(2,1)S(1)}, pred[4,512,1024]{2,1,0:T(32,128)(4,1)S(1)}, bf16[4,512,32]{2,1,0:T(8,128)(2,1)S(1)}, bf16[...) while((s32[]{:T(128)}, bf16[4,512,32]{1,2,0:T(8,128)(2,1)S(1)}, ...), condition=%wide.region_15.15_spmd, body=%wide.region_12.14_spmd.sunk | while | flops 71318528 | bytes 7515217 | solution.py:186
  169.7 1.1 dynamic-slice_bitcast_fusion.5
  170.8 0.9 constant_dynamic-slice_fusion.2
  172.0 1.5 compare_and_fusion.3
  173.5 6.9 %while.35 = (s32[]{:T(128)}, bf16[4,512,32]{1,2,0:T(8,128)(2,1)S(1)}, pred[4,512,1024]{2,1,0:T(32,128)(4,1)S(1)}, bf16[4,512,32]{2,1,0:T(8,128)(2,1)S(1)}, bf16[...) while((s32[]{:T(128)}, bf16[4,512,32]{1,2,0:T(8,128)(2,1)S(1)}, ...), condition=%wide.region_15.15_spmd, body=%wide.region_12.14_spmd.sunk | while | flops 71318528 | bytes 7515217 | solution.py:186
  181.6 1.1 dynamic-slice_bitcast_fusion.5
  182.6 0.9 constant_dynamic-slice_fusion.2
  183.8 1.5 compare_and_fusion.3
  185.4 6.9 %while.35 = (s32[]{:T(128)}, bf16[4,512,32]{1,2,0:T(8,128)(2,1)S(1)}, pred[4,512,1024]{2,1,0:T(32,128)(4,1)S(1)}, bf16[4,512,32]{2,1,0:T(8,128)(2,1)S(1)}, bf16[...) while((s32[]{:T(128)}, bf16[4,512,32]{1,2,0:T(8,128)(2,1)S(1)}, ...), condition=%wide.region_15.15_spmd, body=%wide.region_12.14_spmd.sunk | while | flops 71318528 | bytes 7515217 | solution.py:186
  193.4 1.1 dynamic-slice_bitcast_fusion.5
  194.5 0.9 constant_dynamic-slice_fusion.2
  195.7 1.5 compare_and_fusion.3
  197.2 6.9 %while.35 = (s32[]{:T(128)}, bf16[4,512,32]{1,2,0:T(8,128)(2,1)S(1)}, pred[4,512,1024]{2,1,0:T(32,128)(4,1)S(1)}, bf16[4,512,32]{2,1,0:T(8,128)(2,1)S(1)}, bf16[...) while((s32[]{:T(128)}, bf16[4,512,32]{1,2,0:T(8,128)(2,1)S(1)}, ...), condition=%wide.region_15.15_spmd, body=%wide.region_12.14_spmd.sunk | while | flops 71318528 | bytes 7515217 | solution.py:186
  205.2 5.1 %copy.143 = bf16[5,2048,32]{2,0,1:T(8,128)(2,1)} copy(bf16[5,2048,32]{2,1,0:T(8,128)(2,1)} %get-tuple-element.97) | data formatting | bytes 1310720 | tf_op jit(solution)/shard_map/while | solution.py:195
  210.3 5.4 %reshape.194 = bf16[64,2,2560]{2,1,0:T(2,128)(2,1)S(1)} reshape(bf16[2048,1,5,32]{3,2,1,0:T(8,128)(2,1)} %bitcast.147) | data formatting | bytes 1310720
  215.7 32.1 %all_to_all.84 = bf16[64,2,2560]{2,1,0:T(2,128)(2,1)S(1)} all-to-all(bf16[64,2,2560]{2,1,0:T(2,128)(2,1)S(1)} %reshape.194), channel_id=1, replica_groups=mesh['rows'=64,'feat'=4] {'rows'}, dimensions={0} | all-to-all | bytes 1310720 | tf_op jit(solution)/shard_map/all_to_all | solution.py:196
  247.8 4.0 %reshape.195 = bf16[2048,1,5,32]{3,2,1,0:T(8,128)(2,1)} reshape(bf16[64,2,2560]{2,1,0:T(2,128)(2,1)S(1)} %all_to_all.84) | data formatting | bytes 1310720
  251.8 5.3 %copy.142 = bf16[64,32,1,5,32]{4,3,0,1,2:T(8,128)(2,1)} copy(bf16[64,32,1,5,32]{4,3,1,0,2:T(8,128)(2,1)} %bitcast.148) | data formatting | bytes 1310720 | tf_op jit(solution)/shard_map/all_to_all | solution.py:196
  257.1 4.7 %reshape.171 = bf16[32,80,128]{2,1,0:T(8,128)(2,1)S(1)} reshape(bf16[32,64,1,5,32]{4,3,1,0,2:T(8,128)(2,1)} %bitcast.149) | data formatting | bytes 1310720 | tf_op jit(solution)/shard_map/reshape | solution.py:197
  261.8 1.2 fusion.33
  (160 shorter events, 56.5 us)
Async XLA Ops:
  0.0 48.6 %copy-start = (bf16[128,384]{1,0:T(8,128)(2,1)S(1)}, bf16[128,384]{1,0:T(8,128)(2,1)}, u32[]{:S(2)}) copy-start(bf16[128,384]{1,0:T(8,128)(2,1)} %param.18) | copy-start | bytes 294916
  0.0 31.4 %copy-start.4 = (bf16[128,20,128]{2,0,1:T(8,128)(2,1)S(1)}, bf16[128,20,128]{2,0,1:T(8,128)(2,1)}, u32[]{:S(2)}) copy-start(bf16[128,20,128]{2,0,1:T(8,128)(2,1)} %param.14) | copy-start | bytes 1966084
  7.5 23.3 %all-to-all-start = ((f32[64,1,328]{2,1,0:T(1,128)}), f32[64,1,328]{2,1,0:T(1,128)S(1)}, u32[]{:S(2)}, u32[]{:S(2)}) async-start(f32[64,1,328]{2,1,0:T(1,128)} %broadcast_in_dim.81), calls=%async_computation | async-start | bytes 196608 | tf_op jit(solution)/shard_map/all_to_all | solution.py:16
  32.7 15.7 %all-to-all-start.1 = ((bf16[128,20,128]{2,1,0:T(8,128)(2,1)}), bf16[128,20,128]{2,1,0:T(8,128)(2,1)S(1)}, u32[]{:S(2)}, u32[]{:S(2)}) async-start(bf16[128,20,128]{2,1,0:T(8,128)(2,1)} %fusion.31), calls=%async_computation.1 | async-start | bytes 1572864 | tf_op jit(solution)/shard_map/all_to_all | solution.py:127
  52.2 10.6 %copy-start.7 = (bf16[128,128]{1,0:T(8,128)(2,1)S(1)}, bf16[128,128]{1,0:T(8,128)(2,1)}, u32[]{:S(2)}) copy-start(bf16[128,128]{1,0:T(8,128)(2,1)} %param.19) | copy-start | bytes 98308
  52.8 3.4 %copy-start.5 = (bf16[2,16,80,4,32]{2,4,3,1,0:T(8,128)(2,1)S(1)}, bf16[2,16,80,4,32]{2,4,3,1,0:T(8,128)(2,1)}, u32[]{:S(2)}) copy-start(bf16[2,16,80,4,32]{2,4,3,1,0:T(8,128)(2,1)} %get-tuple-element.407) | copy-start | bytes 1966084 | tf_op jit(solution)/shard_map/while
  58.1 3.4 %copy-start.5 = (bf16[2,16,80,4,32]{2,4,3,1,0:T(8,128)(2,1)S(1)}, bf16[2,16,80,4,32]{2,4,3,1,0:T(8,128)(2,1)}, u32[]{:S(2)}) copy-start(bf16[2,16,80,4,32]{2,4,3,1,0:T(8,128)(2,1)} %get-tuple-element.407) | copy-start | bytes 1966084 | tf_op jit(solution)/shard_map/while
  62.8 2.3 copy-start.6
  64.6 13.6 %copy-start.2 = (bf16[32,80,128]{2,1,0:T(8,128)(2,1)}, bf16[32,80,128]{2,1,0:T(8,128)(2,1)S(1)}, u32[]{:S(2)}) copy-start(bf16[32,80,128]{2,1,0:T(8,128)(2,1)S(1)} %fusion.32) | copy-start | bytes 1966084
  67.1 23.1 %all-to-all-start.3 = ((bf16[64,2,320]{2,1,0:T(2,128)(2,1)}), bf16[64,2,320]{2,1,0:T(2,128)(2,1)S(1)}, u32[]{:S(2)}, u32[]{:S(2)}) async-start(bf16[64,2,320]{2,1,0:T(2,128)(2,1)} %reshape.192), calls=%async_computation.3 | async-start | bytes 196608 | tf_op jit(solution)/shard_map/all_to_all | solution.py:167
  90.2 20.5 %all-to-all-start.4 = ((bf16[64,2,320]{2,1,0:T(2,128)(2,1)}), bf16[64,2,320]{2,1,0:T(2,128)(2,1)S(1)}, u32[]{:S(2)}, u32[]{:S(2)}) async-start(bf16[64,2,320]{2,1,0:T(2,128)(2,1)} %reshape.190), calls=%async_computation.4 | async-start | bytes 196608 | tf_op jit(solution)/shard_map/all_to_all | solution.py:168
  110.7 24.6 %all-to-all-start.2 = ((bf16[64,2,2560]{2,1,0:T(2,128)(2,1)}), bf16[64,2,2560]{2,1,0:T(2,128)(2,1)S(1)}, u32[]{:S(2)}, u32[]{:S(2)}) async-start(bf16[64,2,2560]{2,1,0:T(2,128)(2,1)} %reshape.188), calls=%async_computation.2 | async-start | bytes 1310720 | tf_op jit(solution)/shard_map/all_to_all | solution.py:166
  257.1 4.7 %copy-start.3 = (bf16[32,80,128]{2,1,0:T(8,128)(2,1)S(1)}, bf16[32,80,128]{2,1,0:T(8,128)(2,1)}, u32[]{:S(2)}) copy-start(bf16[32,80,128]{2,1,0:T(8,128)(2,1)} %copy-done.2) | copy-start | bytes 1966084
  257.1 4.7 %copy-start.8 = (bf16[128,128]{1,0:T(8,128)(2,1)S(1)}, bf16[128,128]{1,0:T(8,128)(2,1)}, u32[]{:S(2)}) copy-start(bf16[128,128]{1,0:T(8,128)(2,1)} %param.21) | copy-start | bytes 98308
  257.1 5.9 %copy-start.1 = (bf16[128,384]{1,0:T(8,128)(2,1)S(1)}, bf16[128,384]{1,0:T(8,128)(2,1)}, u32[]{:S(2)}) copy-start(bf16[128,384]{1,0:T(8,128)(2,1)} %param.18) | copy-start | bytes 294916
where the time goes:
time: 264 us; the launch traced here: 263 us
  local copies, waits for them, and re-layouts  85.9 us (33%)
  blocking collectives  43.3 us (16%)
  starting transfers between devices  41.4 us (16%)
  other arithmetic  33.3 us (13%)
  matrix products  31.7 us (12%)
  waiting for transfers between devices  23.7 us (9%)
  between operations  3.17 us (1%)
    all_to_all x1, blocking collectives, on_device(): lax.all_to_all(result, 'rows', split_axis=0, concat_axis=1, tiled=True)  32.1 us
    unnamed x26, local copies, waits for them, and re-layouts  18.4 us
    all_to_all x1, starting transfers between devices, from_everyone(): lax.all_to_all(jnp.broadcast_to(shard[None], (peers, *shard.shape)), axis...  13.1 us
    dot_general x20, matrix products, one_one_block(): jnp.dot(block_query, single_key.T, preferred_element_type=jnp.float32)  12 us
    dot_general x20, matrix products, one_one_block(): jnp.dot(shares, single_value, preferred_element_type=jnp.float32)  12 us
    all_to_all x1, waiting for transfers between devices, on_device(): lax.all_to_all(normed, 'feat', split_axis=0, concat_axis=1, tiled=True)  11.7 us
    all_gather x1, blocking collectives, gather_together(): lines, at, done = (lax.all_gather(vector, axis), 0, [])  11.3 us
    reduce_sum x20, other arithmetic, one_one_block(): shares = jax.nn.softmax(scores, axis=-1).astype(jnp.bfloat16)  10.3 us
  transfers between devices with their start and end apart: 5, of which 4 were waited for; matrix products, arithmetic and copies ran while one was open for 11% of the time, Pallas kernels for 0%

commit v1 on v0

--- a/solution.py
+++ b/solution.py
@@ -193,7 +193,15 @@
         jnp.moveaxis(every_value[:, 0], 1, 0),
     )
     result = jnp.moveaxis(lax.map(one_item, by_item), 0, 1)[:, None]
-    attended = lax.all_to_all(result, "rows", split_axis=0, concat_axis=1, tiled=True)
+    attended = jnp.concatenate(
+        lax.all_to_all(
+            jnp.stack(jnp.split(result, lax.axis_size("rows"), 0)),
+            concat_axis=0,
+            axis_name="rows",
+            split_axis=0,
+        ),
+        1,
+    )
     attended = attended.reshape(group_rows, total_feats, width_all)
     update = jnp.dot(attended, item_out, preferred_element_type=jnp.float32)
     return (mixed_rows.astype(jnp.float32) + update).astype(jnp.bfloat16)

time: 264 us -> 282 us (1.068)
  local copies, waits for them, and re-layouts: 85.9 us -> 101 us
    unnamed x26 -> x89, local copies, waits for them, and re-layouts: 18.4 us -> 40.2 us
    all_to_all x1 -> x0, local copies, waits for them, and re-layouts: 5.32 us -> none  [on_device(): lax.all_to_all(result, 'rows', split_axis=0, concat_axis=1, tiled=True)]
    while x5 -> x4, local copies, waits for them, and re-layouts: 5.07 us -> 0.01 us  [the longest x1 5.06 us: on_device(): result = jnp.moveaxis(lax.map(one_item, by_item), 0, 1)[:, None]]
    another operation x2 -> x4, local copies, waits for them, and re-layouts: 0.86 us -> 5.56 us  [the longest x1 4.69 us: on_device(): attended = attended.reshape(group_rows, total_feats, width_all)]
  transfers between devices with their start and end apart: 5 -> 5, of which waited for: 4 -> 4; matrix products, arithmetic and copies ran while one was open for 11% -> 10% of each run, Pallas kernels for 0% -> 0%
where the time goes in v1:
time: 282 us; the launch traced here: 279 us
  local copies, waits for them, and re-layouts  101 us (36%)
  blocking collectives  43.2 us (15%)
  starting transfers between devices  41.3 us (15%)
  other arithmetic  34.3 us (12%)
  matrix products  31.7 us (11%)
  waiting for transfers between devices  23.8 us (8%)
  between operations  3.23 us (1%)
    unnamed x89, local copies, waits for them, and re-layouts  40.2 us
    all_to_all x1, blocking collectives, on_device(): lax.all_to_all(jnp.stack(jnp.split(result, lax.axis_size('rows'), 0)), co...  31.9 us
    all_to_all x1, starting transfers between devices, from_everyone(): lax.all_to_all(jnp.broadcast_to(shard[None], (peers, *shard.shape)), axis...  13.1 us
    dot_general x20, matrix products, one_one_block(): jnp.dot(block_query, single_key.T, preferred_element_type=jnp.float32)  12 us
    dot_general x20, matrix products, one_one_block(): jnp.dot(shares, single_value, preferred_element_type=jnp.float32)  12 us
    all_to_all x1, waiting for transfers between devices, on_device(): lax.all_to_all(normed, 'feat', split_axis=0, concat_axis=1, tiled=True)  11.7 us
    all_gather x1, blocking collectives, gather_together(): lines, at, done = (lax.all_gather(vector, axis), 0, [])  11.3 us
    all_to_all x1, starting transfers between devices, on_device(): lax.all_to_all(item_value, 'rows', split_axis=1, concat_axis=0, tiled=True)  10.3 us
  transfers between devices with their start and end apart: 5, of which 4 were waited for; matrix products, arithmetic and copies ran while one was open for 10% of the time, Pallas kernels for 0%

profile of v1, /device:TPU:1, one launch (start us, length us, event | category | flops | bytes accessed | tf_op | source)
XLA Modules:
  0.0 278.9 jit_solution(13271201226486438464)
XLA Ops:
  0.0 1.3 dynamic_slice.46
  2.0 1.4 fusion.48
  3.4 1.7 fusion.27
  7.4 13.1 %all-to-all-start = ((f32[64,1,328]{2,1,0:T(1,128)}), f32[64,1,328]{2,1,0:T(1,128)S(1)}, u32[]{:S(2)}, u32[]{:S(2)}) async-start(f32[64,1,328]{2,1,0:T(1,128)} %broadcast_in_dim.52), calls=%async_computation | async-start | bytes 196608 | tf_op jit(solution)/shard_map/all_to_all | solution.py:16
  20.6 0.9 reshape.297
  22.5 1.2 reduce_sum.80
  28.5 2.2 all-to-all-done
  31.2 2.4 fusion.31
  33.7 4.0 %all-to-all-start.1 = ((bf16[128,20,128]{2,1,0:T(8,128)(2,1)}), bf16[128,20,128]{2,1,0:T(8,128)(2,1)S(1)}, u32[]{:S(2)}, u32[]{:S(2)}) async-start(bf16[128,20,128]{2,1,0:T(8,128)(2,1)} %fusion.31), calls=%async_computation.1 | async-start | bytes 1572864 | tf_op jit(solution)/shard_map/all_to_all | solution.py:127
  37.7 11.7 %all-to-all-done.1 = bf16[128,20,128]{2,1,0:T(8,128)(2,1)S(1)} async-done(((bf16[128,20,128]{2,1,0:T(8,128)(2,1)}), bf16[128,20,128]{2,1,0:T(8,128)(2,1)S(1)}, u32[]{:S(2)}, u32[]{:S(2)}) %all-to-all-start.1) | async-done | bytes 655392 | tf_op jit(solution)/shard_map/all_to_all | solution.py:127
  50.5 1.3 copy.104
  53.2 10.6 %while.32 = (s32[]{:T(128)}, bf16[2,16,80,4,32]{2,4,3,1,0:T(8,128)(2,1)}, bf16[2,16,80,4,32]{2,4,3,1,0:T(8,128)(2,1)}, bf16[2,16,80,4,32]{2,4,3,1,0:T(8,128)(2,1...) while((s32[]{:T(128)}, bf16[2,16,80,4,32]{2,4,3,1,0:T(8,128)(2,1)}, ...), condition=%wide.region_7.8_spmd, body=%wide.region_4.7_spmd.sunk | while | flops 55050320 | bytes 12310625 | solution.py:86
  53.7 3.4 %fusion.75 = (f32[16,4,80]{2,1,0:T(4,128)S(1)}, f32[16,4,80,80]{2,3,1,0:T(8,128)S(1)}) fusion(f32[16,4,80,80]{2,3,1,0:T(8,128)S(1)} %fusion.74), kind=kOutput, calls=%fused_computation.216.clone.1 | output fusion | flops 1638479 | bytes 3297280 | tf_op jit(solution)/shard_map/while/body/eval_jaxpr/sub | solution.py:78
  57.2 1.3 fusion.76
  59.0 3.4 %fusion.75 = (f32[16,4,80]{2,1,0:T(4,128)S(1)}, f32[16,4,80,80]{2,3,1,0:T(8,128)S(1)}) fusion(f32[16,4,80,80]{2,3,1,0:T(8,128)S(1)} %fusion.74), kind=kOutput, calls=%fused_computation.216.clone.1 | output fusion | flops 1638479 | bytes 3297280 | tf_op jit(solution)/shard_map/while/body/eval_jaxpr/sub | solution.py:78
  62.5 1.3 fusion.76
  63.7 1.7 fusion.32
  67.1 0.9 reshape.319
  68.0 9.3 %all-to-all-start.3 = ((bf16[64,2,320]{2,1,0:T(2,128)(2,1)}), bf16[64,2,320]{2,1,0:T(2,128)(2,1)S(1)}, u32[]{:S(2)}, u32[]{:S(2)}) async-start(bf16[64,2,320]{2,1,0:T(2,128)(2,1)} %reshape.319), calls=%async_computation.3 | async-start | bytes 196608 | tf_op jit(solution)/shard_map/all_to_all | solution.py:167
  78.0 0.9 reshape.317
  79.3 3.8 %reshape.291 = bf16[32,64,5,32]{3,2,1,0:T(8,128)(2,1)} reshape(bf16[32,80,128]{2,1,0:T(8,128)(2,1)S(1)} %convolution_convert_fusion.2) | data formatting | bytes 1310720 | tf_op jit(solution)/shard_map/reshape | solution.py:144
  83.0 5.2 %copy.137 = bf16[32,64,5,32]{3,0,2,1:T(8,128)(2,1)S(1)} copy(bf16[32,64,5,32]{3,2,1,0:T(8,128)(2,1)} %reshape.291) | data formatting | bytes 1310720 | tf_op jit(solution)/shard_map/reshape | solution.py:144
  88.3 2.6 reshape.315
  90.9 10.3 %all-to-all-start.4 = ((bf16[64,2,320]{2,1,0:T(2,128)(2,1)}), bf16[64,2,320]{2,1,0:T(2,128)(2,1)S(1)}, u32[]{:S(2)}, u32[]{:S(2)}) async-start(bf16[64,2,320]{2,1,0:T(2,128)(2,1)} %reshape.317), calls=%async_computation.4 | async-start | bytes 196608 | tf_op jit(solution)/shard_map/all_to_all | solution.py:168
  102.0 9.4 %all-to-all-done.4 = bf16[64,2,320]{2,1,0:T(2,128)(2,1)S(1)} async-done(((bf16[64,2,320]{2,1,0:T(2,128)(2,1)}), bf16[64,2,320]{2,1,0:T(2,128)(2,1)S(1)}, u32[]{:S(2)}, u32[]{:S(2)}) %all-to-all-start.4) | async-done | bytes 81952 | tf_op jit(solution)/shard_map/all_to_all | solution.py:168
  111.4 4.5 %all-to-all-start.2 = ((bf16[64,2,2560]{2,1,0:T(2,128)(2,1)}), bf16[64,2,2560]{2,1,0:T(2,128)(2,1)S(1)}, u32[]{:S(2)}, u32[]{:S(2)}) async-start(bf16[64,2,2560]{2,1,0:T(2,128)(2,1)} %reshape.315), calls=%async_computation.2 | async-start | bytes 1310720 | tf_op jit(solution)/shard_map/all_to_all | solution.py:166
  116.6 11.3 %all-gather = bf16[327680]{0:T(1024)(128)(2,1)S(1)} all-gather(bf16[81920]{0:T(1024)(128)(2,1)S(1)} %pad_maximum_fusion), channel_id=2, replica_groups=mesh['rows'=64,'feat'=4] {'feat'}, dimensions={0}, use_global_device_ids=true | all-gather | bytes 819200 | tf_op jit(solution)/shard_map/all_gather | solution.py:43
  128.1 1.0 fusion.52
  129.1 2.3 squeeze_reshape_reshape.6
  131.4 1.3 copy.117
  132.7 1.4 squeeze_reshape_reshape.7
  134.1 1.3 copy.118
  136.0 1.4 reshape.316
  137.4 2.0 bitcast_bitcast_fusion.1
  139.3 3.9 %copy.109 = bf16[64,32,1,5,32]{1,0,4,3,2:T(8,128)(2,1)S(1)} copy(bf16[64,32,1,5,32]{4,1,3,0,2:T(8,128)(2,1)} %bitcast_bitcast_fusion.1) | data formatting | bytes 1310720 | tf_op jit(solution)/shard_map/all_to_all | solution.py:166
  143.2 3.5 %squeeze.38 = bf16[2048,5,32]{0,2,1:T(8,128)(2,1)} reshape(bf16[64,32,1,5,32]{1,0,4,3,2:T(8,128)(2,1)S(1)} %copy.109) | data formatting | bytes 1310720 | tf_op jit(solution)/shard_map/squeeze | solution.py:191
  146.7 59.1 %while.34 = (s32[]{:T(128)}, bf16[5,2048,32]{2,1,0:T(8,128)(2,1)}, bf16[5,2048,32]{1,2,0:T(8,128)(2,1)}, bf16[5,1024,32]{2,1,0:T(8,128)(2,1)}, bf16[5,1024,32]{2...) while((s32[]{:T(128)}, bf16[5,2048,32]{2,1,0:T(8,128)(2,1)}, ...), condition=%wide.region_16.17_spmd.clone, body=%wide.region_11.16_spmd.clone.sunk | while | flops 75512832 | bytes 11330310 | solution.py:195
  146.7 1.1 dynamic-slice_bitcast_fusion.5
  147.8 0.9 constant_dynamic-slice_fusion.2
  149.0 1.5 compare_and_fusion.3
  150.5 6.9 %while.35 = (s32[]{:T(128)}, bf16[4,512,32]{1,2,0:T(8,128)(2,1)S(1)}, pred[4,512,1024]{2,1,0:T(32,128)(4,1)S(1)}, bf16[4,512,32]{2,1,0:T(8,128)(2,1)S(1)}, bf16[...) while((s32[]{:T(128)}, bf16[4,512,32]{1,2,0:T(8,128)(2,1)S(1)}, ...), condition=%wide.region_15.15_spmd, body=%wide.region_12.14_spmd.sunk | while | flops 71318528 | bytes 7515217 | solution.py:186
  158.5 1.1 dynamic-slice_bitcast_fusion.5
  159.6 0.9 constant_dynamic-slice_fusion.2
  160.8 1.5 compare_and_fusion.3
  162.4 6.9 %while.35 = (s32[]{:T(128)}, bf16[4,512,32]{1,2,0:T(8,128)(2,1)S(1)}, pred[4,512,1024]{2,1,0:T(32,128)(4,1)S(1)}, bf16[4,512,32]{2,1,0:T(8,128)(2,1)S(1)}, bf16[...) while((s32[]{:T(128)}, bf16[4,512,32]{1,2,0:T(8,128)(2,1)S(1)}, ...), condition=%wide.region_15.15_spmd, body=%wide.region_12.14_spmd.sunk | while | flops 71318528 | bytes 7515217 | solution.py:186
  170.4 1.1 dynamic-slice_bitcast_fusion.5
  171.4 0.9 constant_dynamic-slice_fusion.2
  172.6 1.5 compare_and_fusion.3
  174.2 6.9 %while.35 = (s32[]{:T(128)}, bf16[4,512,32]{1,2,0:T(8,128)(2,1)S(1)}, pred[4,512,1024]{2,1,0:T(32,128)(4,1)S(1)}, bf16[4,512,32]{2,1,0:T(8,128)(2,1)S(1)}, bf16[...) while((s32[]{:T(128)}, bf16[4,512,32]{1,2,0:T(8,128)(2,1)S(1)}, ...), condition=%wide.region_15.15_spmd, body=%wide.region_12.14_spmd.sunk | while | flops 71318528 | bytes 7515217 | solution.py:186
  182.2 1.1 dynamic-slice_bitcast_fusion.5
  183.3 0.9 constant_dynamic-slice_fusion.2
  184.5 1.5 compare_and_fusion.3
  186.0 6.9 %while.35 = (s32[]{:T(128)}, bf16[4,512,32]{1,2,0:T(8,128)(2,1)S(1)}, pred[4,512,1024]{2,1,0:T(32,128)(4,1)S(1)}, bf16[4,512,32]{2,1,0:T(8,128)(2,1)S(1)}, bf16[...) while((s32[]{:T(128)}, bf16[4,512,32]{1,2,0:T(8,128)(2,1)S(1)}, ...), condition=%wide.region_15.15_spmd, body=%wide.region_12.14_spmd.sunk | while | flops 71318528 | bytes 7515217 | solution.py:186
  194.0 1.1 dynamic-slice_bitcast_fusion.5
  195.1 0.9 constant_dynamic-slice_fusion.2
  196.3 1.5 compare_and_fusion.3
  197.9 6.9 %while.35 = (s32[]{:T(128)}, bf16[4,512,32]{1,2,0:T(8,128)(2,1)S(1)}, pred[4,512,1024]{2,1,0:T(32,128)(4,1)S(1)}, bf16[4,512,32]{2,1,0:T(8,128)(2,1)S(1)}, bf16[...) while((s32[]{:T(128)}, bf16[4,512,32]{1,2,0:T(8,128)(2,1)S(1)}, ...), condition=%wide.region_15.15_spmd, body=%wide.region_12.14_spmd.sunk | while | flops 71318528 | bytes 7515217 | solution.py:186
  205.9 0.9 constant_dynamic-update-slice_fusion.63
  231.7 1.9 reshape.321
  233.7 31.9 %all_to_all.74 = bf16[64,2,2560]{2,1,0:T(2,128)(2,1)} all-to-all(bf16[64,2,2560]{2,1,0:T(2,128)(2,1)S(1)} %reshape.321), channel_id=1, replica_groups=mesh['rows'=64,'feat'=4] {'rows'}, dimensions={0} | all-to-all | bytes 1310720 | tf_op jit(solution)/shard_map/all_to_all | solution.py:197
  265.6 3.6 %reshape.322 = bf16[64,1,5,32,32]{4,3,2,1,0:T(8,128)(2,1)S(1)} reshape(bf16[64,2,2560]{2,1,0:T(2,128)(2,1)} %all_to_all.74) | data formatting | bytes 1310720
  269.7 3.3 %copy.119 = bf16[32,64,1,5,32]{4,3,1,0,2:T(8,128)(2,1)} copy(bf16[32,64,1,5,32]{4,0,3,2,1:T(8,128)(2,1)S(1)} %bitcast_bitcast_fusion) | data formatting | bytes 1310720 | tf_op jit(solution)/shard_map/reshape | solution.py:196
  273.0 4.7 %reshape_reshape.15 = bf16[32,80,128]{2,1,0:T(8,128)(2,1)S(1)} reshape(bf16[32,64,1,5,32]{4,3,1,0,2:T(8,128)(2,1)} %copy.119) | data formatting | bytes 1310720 | tf_op jit(solution)/shard_map/reshape;reshape | solution.py:205
  277.7 1.2 fusion.33
  (224 shorter events, 81.6 us)
Async XLA Ops:
  0.0 49.5 %copy-start = (bf16[128,384]{1,0:T(8,128)(2,1)S(1)}, bf16[128,384]{1,0:T(8,128)(2,1)}, u32[]{:S(2)}) copy-start(bf16[128,384]{1,0:T(8,128)(2,1)} %param.18) | copy-start | bytes 294916
  7.4 23.3 %all-to-all-start = ((f32[64,1,328]{2,1,0:T(1,128)}), f32[64,1,328]{2,1,0:T(1,128)S(1)}, u32[]{:S(2)}, u32[]{:S(2)}) async-start(f32[64,1,328]{2,1,0:T(1,128)} %broadcast_in_dim.52), calls=%async_computation | async-start | bytes 196608 | tf_op jit(solution)/shard_map/all_to_all | solution.py:16
  33.7 15.7 %all-to-all-start.1 = ((bf16[128,20,128]{2,1,0:T(8,128)(2,1)}), bf16[128,20,128]{2,1,0:T(8,128)(2,1)S(1)}, u32[]{:S(2)}, u32[]{:S(2)}) async-start(bf16[128,20,128]{2,1,0:T(8,128)(2,1)} %fusion.31), calls=%async_computation.1 | async-start | bytes 1572864 | tf_op jit(solution)/shard_map/all_to_all | solution.py:127
  53.1 10.6 %copy-start.7 = (bf16[128,128]{1,0:T(8,128)(2,1)S(1)}, bf16[128,128]{1,0:T(8,128)(2,1)}, u32[]{:S(2)}) copy-start(bf16[128,128]{1,0:T(8,128)(2,1)} %param.19) | copy-start | bytes 98308
  53.1 12.9 %copy-start.6 = (bf16[128,384]{1,0:T(8,128)(2,1)S(1)}, bf16[128,384]{1,0:T(8,128)(2,1)}, u32[]{:S(2)}) copy-start(bf16[128,384]{1,0:T(8,128)(2,1)} %param.20) | copy-start | bytes 294916
  53.7 3.4 %copy-start.5 = (bf16[2,16,80,4,32]{2,4,3,1,0:T(8,128)(2,1)S(1)}, bf16[2,16,80,4,32]{2,4,3,1,0:T(8,128)(2,1)}, u32[]{:S(2)}) copy-start(bf16[2,16,80,4,32]{2,4,3,1,0:T(8,128)(2,1)} %get-tuple-element.407) | copy-start | bytes 1966084 | tf_op jit(solution)/shard_map/while
  59.0 3.4 %copy-start.5 = (bf16[2,16,80,4,32]{2,4,3,1,0:T(8,128)(2,1)S(1)}, bf16[2,16,80,4,32]{2,4,3,1,0:T(8,128)(2,1)}, u32[]{:S(2)}) copy-start(bf16[2,16,80,4,32]{2,4,3,1,0:T(8,128)(2,1)} %get-tuple-element.407) | copy-start | bytes 1966084 | tf_op jit(solution)/shard_map/while
  65.4 13.8 %copy-start.2 = (bf16[32,80,128]{2,1,0:T(8,128)(2,1)}, bf16[32,80,128]{2,1,0:T(8,128)(2,1)S(1)}, u32[]{:S(2)}) copy-start(bf16[32,80,128]{2,1,0:T(8,128)(2,1)S(1)} %fusion.32) | copy-start | bytes 1966084
  68.0 22.9 %all-to-all-start.3 = ((bf16[64,2,320]{2,1,0:T(2,128)(2,1)}), bf16[64,2,320]{2,1,0:T(2,128)(2,1)S(1)}, u32[]{:S(2)}, u32[]{:S(2)}) async-start(bf16[64,2,320]{2,1,0:T(2,128)(2,1)} %reshape.319), calls=%async_computation.3 | async-start | bytes 196608 | tf_op jit(solution)/shard_map/all_to_all | solution.py:167
  90.9 20.5 %all-to-all-start.4 = ((bf16[64,2,320]{2,1,0:T(2,128)(2,1)}), bf16[64,2,320]{2,1,0:T(2,128)(2,1)S(1)}, u32[]{:S(2)}, u32[]{:S(2)}) async-start(bf16[64,2,320]{2,1,0:T(2,128)(2,1)} %reshape.317), calls=%async_computation.4 | async-start | bytes 196608 | tf_op jit(solution)/shard_map/all_to_all | solution.py:168
  111.4 24.6 %all-to-all-start.2 = ((bf16[64,2,2560]{2,1,0:T(2,128)(2,1)}), bf16[64,2,2560]{2,1,0:T(2,128)(2,1)S(1)}, u32[]{:S(2)}, u32[]{:S(2)}) async-start(bf16[64,2,2560]{2,1,0:T(2,128)(2,1)} %reshape.315), calls=%async_computation.2 | async-start | bytes 1310720 | tf_op jit(solution)/shard_map/all_to_all | solution.py:166
  205.9 25.4 %copy-start.4 = (bf16[5,2048,32]{2,1,0:T(8,128)(2,1)S(1)}, bf16[5,2048,32]{2,1,0:T(8,128)(2,1)}, u32[]{:S(2)}) copy-start(bf16[5,2048,32]{2,1,0:T(8,128)(2,1)} %get-tuple-element.97) | copy-start | bytes 1966084
  269.7 9.2 %copy-start.1 = (bf16[128,384]{1,0:T(8,128)(2,1)S(1)}, bf16[128,384]{1,0:T(8,128)(2,1)}, u32[]{:S(2)}) copy-start(bf16[128,384]{1,0:T(8,128)(2,1)} %param.18) | copy-start | bytes 294916
  273.0 4.7 %copy-start.3 = (bf16[32,80,128]{2,1,0:T(8,128)(2,1)S(1)}, bf16[32,80,128]{2,1,0:T(8,128)(2,1)}, u32[]{:S(2)}) copy-start(bf16[32,80,128]{2,1,0:T(8,128)(2,1)} %copy-done.2) | copy-start | bytes 1966084
  273.0 4.7 %copy-start.8 = (bf16[128,128]{1,0:T(8,128)(2,1)S(1)}, bf16[128,128]{1,0:T(8,128)(2,1)}, u32[]{:S(2)}) copy-start(bf16[128,128]{1,0:T(8,128)(2,1)} %param.21) | copy-start | bytes 98308
